TPU v7x, 32 devices: a whole 2x2x4 slice. The times are simulated.
32 devices in a mesh: row: 8 (over y, x, core), rep: 4 (over z).
Axes of the slice: x: 2, y: 2, z: 4, core: 2. Of those that a mesh axis runs over, the one named last changes fastest.
Arguments:
- features: bfloat16 [8192, 512], P(('row', 'rep')), may hold values from -6 to 6
- tiles: bfloat16 [64, 8, 128, 128], P(('row', 'rep')), may hold values from -0.1875 to 0.1875
- columns: int32 [64, 8], P(('row', 'rep')), may hold values from 0 to 63, as said below
- w_aggregate: bfloat16 [512, 512], replicated, may hold values from -0.25 to 0.25
- w_self: bfloat16 [512, 512], replicated, may hold values from -0.25 to 0.25
- w_middle: bfloat16 [512, 512], replicated, may hold values from -0.25 to 0.25
- w_output: bfloat16 [512, 512], replicated, may hold values from -0.25 to 0.25
- cotangent: bfloat16 [8192, 512], P(('row', 'rep')), may hold values from -6 to 6
Outputs:
- updated: bfloat16 [8192, 512], P(('row', 'rep'))
- grad_features: bfloat16 [8192, 512], P(('row', 'rep'))
- grad_output: float32 [512, 512], P('rep')
- grad_middle: float32 [512, 512], P('rep')
- grad_aggregate: float32 [512, 512], P('rep')
- grad_self: float32 [512, 512], P('rep')
Inputs may be any that keep to these rules, and one draw needn't show every extreme that they name: `columns`: row group g holds row blocks g * 8 to (g + 1) * 8 - 1, for g < 8. Every column block named by a row block of group g lies in group g - 1, g or g + 1, taken modulo 8; every row block names each of these three groups at least once. Column blocks may repeat within a row block.
All inputs are finite; a program needn't handle non-finite values.
Results may differ from a plain program's by a relative error of at most 0.015.
Values may be sent and summed in bfloat16 or wider, within the bound.
No kernel may reach another device: no remote copies, remote signals or barrier semaphores. Data moves between devices by JAX's collectives and lax.ppermute only.
A program may use at most 192 MiB of HBM per device.

v0:
```python
import math
import jax
import jax.numpy as jnp
from jax import lax
from jax.sharding import PartitionSpec as P


def from_behind(value, axis, steps):
    count = lax.axis_size(axis)
    pairs = [(source, (source + steps) % count) for source in range(count)]
    return lax.ppermute(value, axis, pairs)


def silu_slope(value):
    sig = jax.nn.sigmoid(value)
    return sig * (1.0 + value * (1.0 - sig))


def times_transposed(left_operand, weight):
    return lax.dot_general(
        left_operand, weight, (((1,), (1,)), ((), ())), preferred_element_type=jnp.float32
    )


def local(features, tiles, columns, w_aggregate, w_self, w_middle, w_output, cotangent):
    blocks_dev, width_k, tile_size, _ = tiles.shape
    width = features.shape[1]
    groups = lax.axis_size("row")
    replicas = lax.axis_size("rep")
    panel_blocks = replicas * blocks_dev
    panel_rows = panel_blocks * tile_size
    group_id = lax.axis_index("row")
    slot_of = (columns // panel_blocks - group_id + 1) % groups
    window_index = slot_of * panel_blocks + columns % panel_blocks
    own_panel = lax.all_gather(features, "rep", axis=0, tiled=True)
    prior_panel = from_behind(own_panel, "row", 1)
    next_panel = from_behind(own_panel, "row", -1)
    window = jnp.concatenate([prior_panel, own_panel, next_panel], 0).reshape(
        3 * panel_blocks, tile_size, width
    )
    picked = window[window_index]
    summed = jnp.einsum("bkij,bkjf->bif", tiles, picked, preferred_element_type=jnp.float32)
    aggregate = summed.reshape(blocks_dev * tile_size, width).astype(jnp.bfloat16)
    pre_first = jnp.dot(aggregate, w_aggregate, preferred_element_type=jnp.float32) + jnp.dot(
        features, w_self, preferred_element_type=jnp.float32
    )
    first = jax.nn.silu(pre_first).astype(jnp.bfloat16)
    pre_second = jnp.dot(first, w_middle, preferred_element_type=jnp.float32)
    second = jax.nn.silu(pre_second).astype(jnp.bfloat16)
    updated = (
        features.astype(jnp.float32) + jnp.dot(second, w_output, preferred_element_type=jnp.float32)
    ).astype(jnp.bfloat16)
    delta_second = (times_transposed(cotangent, w_output) * silu_slope(pre_second)).astype(
        jnp.bfloat16
    )
    delta_first = (times_transposed(delta_second, w_middle) * silu_slope(pre_first)).astype(
        jnp.bfloat16
    )
    delta_aggregate = times_transposed(delta_first, w_aggregate).astype(jnp.bfloat16)
    delta_blocks = delta_aggregate.reshape(blocks_dev, tile_size, width)
    messages = jnp.einsum("bkji,bjf->bkif", tiles, delta_blocks, preferred_element_type=jnp.float32)
    spread = jnp.zeros((3 * panel_blocks, tile_size, width), jnp.float32)
    spread = spread.at[window_index.reshape(-1)].add(messages.reshape(-1, tile_size, width))
    spread = spread.reshape(3 * panel_rows, width)
    prior_part = spread[:panel_rows]
    own_part = spread[panel_rows : 2 * panel_rows]
    next_part = spread[2 * panel_rows :]
    from_next = from_behind(prior_part.astype(jnp.bfloat16), "row", -1).astype(prior_part.dtype)
    from_prior = from_behind(next_part.astype(jnp.bfloat16), "row", 1).astype(next_part.dtype)
    returned = lax.psum_scatter(
        (own_part + from_next + from_prior).astype(jnp.bfloat16),
        "rep",
        scatter_dimension=0,
        tiled=True,
    ).astype(jnp.float32)
    grad_features = (
        cotangent.astype(jnp.float32) + times_transposed(delta_first, w_self) + returned
    ).astype(jnp.bfloat16)
    total_nodes = features.shape[0] * groups * replicas
    scale = 1.0 / math.sqrt(total_nodes)
    local_output = jnp.dot(second.T, cotangent, preferred_element_type=jnp.float32)
    local_middle = jnp.dot(first.T, delta_second, preferred_element_type=jnp.float32)
    local_aggregate = jnp.dot(aggregate.T, delta_first, preferred_element_type=jnp.float32)
    local_self = jnp.dot(features.T, delta_first, preferred_element_type=jnp.float32)
    shares = (
        lax.psum_scatter(
            local_output.astype(jnp.bfloat16), "rep", scatter_dimension=0, tiled=True
        ).astype(jnp.float32),
        lax.psum_scatter(
            local_middle.astype(jnp.bfloat16), "rep", scatter_dimension=0, tiled=True
        ).astype(jnp.float32),
        lax.psum_scatter(
            local_aggregate.astype(jnp.bfloat16), "rep", scatter_dimension=0, tiled=True
        ).astype(jnp.float32),
        lax.psum_scatter(
            local_self.astype(jnp.bfloat16), "rep", scatter_dimension=0, tiled=True
        ).astype(jnp.float32),
    )
    totals = (
        lax.psum(shares[0].astype(jnp.bfloat16), "row").astype(jnp.float32),
        lax.psum(shares[1].astype(jnp.bfloat16), "row").astype(jnp.float32),
        lax.psum(shares[2].astype(jnp.bfloat16), "row").astype(jnp.float32),
        lax.psum(shares[3].astype(jnp.bfloat16), "row").astype(jnp.float32),
    )
    return (
        updated,
        grad_features,
        totals[0] * scale,
        totals[1] * scale,
        totals[2] * scale,
        totals[3] * scale,
    )


def solution(mesh):
    placed = (
        P(("row", "rep"), None),
        P(("row", "rep"), None, None, None),
        P(("row", "rep"), None),
        P(),
        P(),
        P(),
        P(),
        P(("row", "rep"), None),
    )
    return jax.shard_map(
        local,
        mesh=mesh,
        in_specs=placed,
        out_specs=(
            P(("row", "rep"), None),
            P(("row", "rep"), None),
            P("rep", None),
            P("rep", None),
            P("rep", None),
            P("rep", None),
        ),
        check_vma=False,
    )
```

profile of v0, /device:TPU:0, one launch (start us, length us, event | category | flops | bytes accessed | tf_op | source)
XLA Modules:
  0.0 258.1 jit_solution(4128961649939991356)
XLA Ops:
  7.2 0.0 copy-start
  7.2 0.0 all-gather.2.cloned.1.call-start
  7.2 0.7 all-gather.2.cloned.1.call-update
  7.9 0.0 reduce-scatter.10.cloned.1.call-start
  8.0 32.3 %all-gather.2.cloned.1.call-done = bf16[1024,512]{1,0:T(8,128)(2,1)} async-done(((bf16[256,512]{1,0:T(8,128)(2,1)}), bf16[1024,512]{1,0:T(8,128)(2,1)}) %all-gather.2.cloned.1.call-update) | async-done | bytes 1048592 | tf_op jit(solution)/shard_map/all_gather | solution.py:35
  40.3 1.3 collective-permute-start.1
  41.6 0.7 compare_select_fusion
  42.3 0.1 reshape.66
  42.4 22.6 %collective-permute-done.1 = bf16[1024,512]{1,0:T(8,128)(2,1)S(1)} collective-permute-done((bf16[1024,512]{1,0:T(8,128)(2,1)}, bf16[1024,512]{1,0:T(8,128)(2,1)S(1)}, u32[]{:S(2)}, u32[]{:S(2)}) %collective-permute-start.1) | collective-permute-done | bytes 1048608 | tf_op jit(solution)/shard_map/ppermute | solution.py:11
  65.1 1.8 collective-permute-done
  66.9 2.8 %pad_maximum_fusion = bf16[3072,512]{1,0:T(8,128)(2,1)} fusion(bf16[1024,512]{1,0:T(8,128)(2,1)S(1)} %collective-permute-done.1, bf16[1024,512]{1,0:T(8,128)(2,1)} %all-gather.2.cloned.1.call-done, bf16[1024,512]{1,0:T(8,128)(2,1)S(1)} %collective-permute-done), kind=kLoop, calls=%fused_computation.2 | loop fusion | flops 9437184 | bytes 6291456 | tf_op jit(solution)/shard_map/concatenate | solution.py:38
  69.7 2.6 gather_fusion
  72.3 0.0 copy-start.4
  72.3 0.0 copy-start.1
  72.3 0.0 copy-start.2
  72.3 0.0 copy-start.8
  72.3 0.4 fusion.3
  72.8 0.0 copy-start.6
  72.8 0.5 copy-done.4
  73.3 0.3 fusion.14
  73.6 0.3 convolution_add_fusion.2
  73.9 0.3 fusion.11
  74.3 0.4 fusion.5
  74.7 0.0 copy-start.13
  74.7 0.7 copy-done.13
  75.4 1.2 convolution_convert_fusion.2
  76.6 0.0 reduce-scatter.10.cloned.1.call-update
  76.6 0.0 reduce-scatter.12.cloned.1.call-start
  76.7 1.4 fusion.6
  78.1 0.0 copy-start.5
  78.1 1.1 convolution_convert_fusion.1
  79.2 0.0 reduce-scatter.12.cloned.1.call-update
  79.2 0.0 reduce-scatter.8.cloned.1.call-start
  79.3 0.1 reshape.61
  79.4 1.2 convolution_convert_fusion.3
  80.5 0.0 reduce-scatter.8.cloned.1.call-update
  80.6 0.0 reduce-scatter.14.cloned.1.call-start
  80.6 0.3 convolution_convert_fusion.4
  81.0 2.7 %fusion.15 = f32[2,512,8,128]{3,1,2,0:T(8,128)} fusion(bf16[2,128,512,1]{2,1,3,0:T(8,128)(2,1)S(1)} %bitcast.59, bf16[2,8,128,128]{3,2,1,0:T(8,128)(2,1)S(1)} %copy-done), kind=kOutput, calls=%fused_computation.49 | convolution fusion | flops 268435456 | bytes 4980736 | tf_op jit(solution)/shard_map/bkji,bjf->bkif/dot_general | solution.py:61
  83.6 5.4 %copy.15 = f32[16,128,512]{2,1,0:T(8,128)} copy(f32[16,128,512]{1,2,0:T(8,128)} %bitcast.54) | data formatting | bytes 8388608 | tf_op jit(solution)/shard_map/reshape | solution.py:63
  89.0 3.5 %broadcast_in_dim.8 = f32[24,128,512]{2,1,0:T(8,128)} broadcast(f32[]{:T(128)} %constant.53.clone.1), dimensions={} | broadcast | bytes 6291460 | tf_op jit(solution)/shard_map/broadcast_in_dim | solution.py:62
  92.5 9.6 %scatter_fusion = f32[24,128,512]{2,1,0:T(8,128)} fusion(f32[24,128,512]{2,1,0:T(8,128)} %broadcast_in_dim.8, s32[16]{0:T(128)S(1)} %fusion.10, f32[16,128,512]{2,1,0:T(8,128)} %copy.15), kind=kCustom, calls=%fused_computation.1 | custom fusion | flops 1048576 | bytes 12582976 | tf_op jit(solution)/shard_map/scatter-add | solution.py:63
  102.0 3.4 %convert.4 = bf16[24,128,512]{2,1,0:T(8,128)(2,1)S(1)} convert(f32[24,128,512]{2,1,0:T(8,128)} %scatter_fusion) | non-fusion elementwise | flops 1572864 | bytes 9437184 | tf_op jit(solution)/shard_map/convert.1
  105.4 1.6 fusion.13
  107.0 1.2 fusion.2
  108.2 0.0 reduce-scatter.14.cloned.1.call-update
  108.2 0.0 all-reduce.3.cloned.1.call-start
  108.3 2.7 %collective-permute-start.2 = (bf16[1024,512]{1,0:T(8,128)(2,1)}, bf16[1024,512]{1,0:T(8,128)(2,1)}, u32[]{:S(2)}, u32[]{:S(2)}) collective-permute-start(bf16[1024,512]{1,0:T(8,128)(2,1)} %bitcast.12), channel_id=1, source_target_pairs={{0,28},{4,0},{8,4},{12,8},{16,12},{20,16},{24,20},{28,24},{1,29},{... | collective-permute-start | bytes 3145736 | tf_op jit(solution)/shard_map/ppermute | solution.py:11
  111.0 1.9 slice.22
  112.8 0.0 reduce-scatter.10.cloned.1.call-done
  112.9 6.7 %reduce-scatter.12.cloned.1.call-done = bf16[128,512]{1,0:T(8,128)(2,1)} async-done(((bf16[512,512]{1,0:T(8,128)(2,1)}), bf16[128,512]{1,0:T(8,128)(2,1)}) %reduce-scatter.12.cloned.1.call-update) | async-done | bytes 131088 | tf_op jit(solution)/shard_map/reduce_scatter | solution.py:92
  119.5 22.2 %reduce-scatter.8.cloned.1.call-done = bf16[128,512]{1,0:T(8,128)(2,1)} async-done(((bf16[512,512]{1,0:T(8,128)(2,1)}), bf16[128,512]{1,0:T(8,128)(2,1)}) %reduce-scatter.8.cloned.1.call-update) | async-done | bytes 131088 | tf_op jit(solution)/shard_map/reduce_scatter | solution.py:86
  141.8 22.2 %reduce-scatter.14.cloned.1.call-done = bf16[128,512]{1,0:T(8,128)(2,1)} async-done(((bf16[512,512]{1,0:T(8,128)(2,1)}), bf16[128,512]{1,0:T(8,128)(2,1)}) %reduce-scatter.14.cloned.1.call-update) | async-done | bytes 131088 | tf_op jit(solution)/shard_map/reduce_scatter | solution.py:95
  164.0 0.0 all-reduce.3.cloned.1.call-update
  164.0 0.0 reduce-scatter.6.cloned.1.call-start
  164.1 3.2 %fusion.1 = bf16[1024,512]{1,0:T(8,128)(2,1)} fusion(f32[8,128,512]{2,1,0:T(8,128)S(1)} %slice.22, bf16[1024,512]{1,0:T(8,128)(2,1)} %collective-permute-done.3, bf16[1024,512]{1,0:T(8,128)(2,1)} %collective-permute-done.2), kind=kLoop, calls=%fused_computation.5 | loop fusion | flops 2621440 | bytes 5242880 | tf_op jit(solution)/shard_map/convert_element_type | solution.py:71
  167.3 0.0 reduce-scatter.6.cloned.1.call-update
  167.4 2.3 fusion.4
  169.7 0.3 convolution_add_fusion
  170.0 50.6 %all-reduce.3.cloned.1.call-done = (bf16[128,512]{1,0:T(8,128)(2,1)}, bf16[128,512]{1,0:T(8,128)(2,1)}, bf16[128,512]{1,0:T(8,128)(2,1)}, bf16[128,512]{1,0:T(8,128)(2,1)}) async-done(((bf16[128,512]{1,0:T(8,128)(2,1)}, bf16[128,512]{1,0:T(8,128)(2,1)}, bf16[128,512]{1,0:T(8,128)(2,1)}, bf16[128,512]{1,0:T(8,128)(2,1)}), (bf16[128,512]{1,0:T(8,128)(2,1)}, bf16[128,512]{1,0:T(8,128)(2,1)}, ...) | async-done | bytes 524304 | tf_op jit(solution)/shard_map/psum | solution.py:100
  220.6 1.8 convert_multiply_fusion.2
  222.4 1.8 convert_multiply_fusion
  224.2 25.3 %reduce-scatter.6.cloned.1.call-done = bf16[256,512]{1,0:T(8,128)(2,1)} async-done(((bf16[1024,512]{1,0:T(8,128)(2,1)}), bf16[256,512]{1,0:T(8,128)(2,1)}) %reduce-scatter.6.cloned.1.call-update) | async-done | bytes 262160 | tf_op jit(solution)/shard_map/reduce_scatter | solution.py:70
  249.6 1.7 add_convert_fusion
  (24 shorter events, 0.1 us)
Async XLA Ops:
  7.2 65.1 %copy-start = (bf16[2,8,128,128]{3,2,1,0:T(8,128)(2,1)S(1)}, bf16[2,8,128,128]{3,2,1,0:T(8,128)(2,1)}, u32[]{:S(2)}) copy-start(bf16[2,8,128,128]{3,2,1,0:T(8,128)(2,1)} %param.9) | copy-start | bytes 1572868
  7.2 33.1 %all-gather.2.cloned.1.call-start = ((), (), s32[]{:S(2)}) async-start(), calls=%async_computation.5 | async-start | bytes 1310720 | tf_op jit(solution)/shard_map/all_gather | solution.py:35
  7.9 104.9 %reduce-scatter.10.cloned.1.call-start = ((), (), s32[]{:S(2)}) async-start(), calls=%async_computation.8 | async-start | bytes 655360 | tf_op jit(solution)/shard_map/reduce_scatter | solution.py:89
  40.3 24.8 %collective-permute-start.1 = (bf16[1024,512]{1,0:T(8,128)(2,1)}, bf16[1024,512]{1,0:T(8,128)(2,1)S(1)}, u32[]{:S(2)}, u32[]{:S(2)}) collective-permute-start(bf16[1024,512]{1,0:T(8,128)(2,1)} %all-gather.2.cloned.1.call-done), channel_id=1, source_target_pairs={{0,28},{4,0},{8,4},{12,8},{16,12},{20,16},{24,20},{28,24},{1,29},{... | collective-permute-start | bytes 3145736 | tf_op jit(solution)/shard_map/ppermute | solution.py:11
  41.6 25.3 %collective-permute-start = (bf16[1024,512]{1,0:T(8,128)(2,1)}, bf16[1024,512]{1,0:T(8,128)(2,1)S(1)}, u32[]{:S(2)}, u32[]{:S(2)}) collective-permute-start(bf16[1024,512]{1,0:T(8,128)(2,1)} %all-gather.2.cloned.1.call-done), channel_id=1, source_target_pairs={{0,4},{4,8},{8,12},{12,16},{16,20},{20,24},{24,28},{28,0},{1,5},{5... | collective-permute-start | bytes 3145736 | tf_op jit(solution)/shard_map/ppermute | solution.py:11
  72.3 1.0 copy-start.4
  72.3 1.3 copy-start.1
  72.3 1.3 copy-start.2
  72.3 1.6 copy-start.8
  72.8 1.5 copy-start.6
  72.8 1.5 copy-start.10
  74.3 2.3 copy-start.11
  74.3 2.4 copy-start.9
  74.7 0.7 copy-start.13
  76.6 2.8 %copy-start.12 = (f32[256,512]{1,0:T(8,128)S(1)}, f32[256,512]{1,0:T(8,128)}, u32[]{:S(2)}) copy-start(f32[256,512]{1,0:T(8,128)} %copy-done.11) | copy-start | bytes 1572868
  76.6 43.0 %reduce-scatter.12.cloned.1.call-start = ((), (), s32[]{:S(2)}) async-start(), calls=%async_computation.9 | async-start | bytes 655360 | tf_op jit(solution)/shard_map/reduce_scatter | solution.py:92
  78.1 2.5 copy-start.5
  79.2 62.6 %reduce-scatter.8.cloned.1.call-start = ((), (), s32[]{:S(2)}) async-start(), calls=%async_computation.7 | async-start | bytes 655360 | tf_op jit(solution)/shard_map/reduce_scatter | solution.py:86
  80.6 83.5 %reduce-scatter.14.cloned.1.call-start = ((), (), s32[]{:S(2)}) async-start(), calls=%async_computation.10 | async-start | bytes 655360 | tf_op jit(solution)/shard_map/reduce_scatter | solution.py:95
  107.0 57.1 %collective-permute-start.3 = (bf16[1024,512]{1,0:T(8,128)(2,1)}, bf16[1024,512]{1,0:T(8,128)(2,1)}, u32[]{:S(2)}, u32[]{:S(2)}) collective-permute-start(bf16[1024,512]{1,0:T(8,128)(2,1)} %bitcast.13), channel_id=1, source_target_pairs={{0,4},{4,8},{8,12},{12,16},{16,20},{20,24},{24,28},{28,0},{1,5},{5... | collective-permute-start | bytes 3145736 | tf_op jit(solution)/shard_map/ppermute | solution.py:11
  108.2 112.4 %all-reduce.3.cloned.1.call-start = ((), (), s32[]{:S(2)}) async-start(), calls=%async_computation.11 | async-start | bytes 1048576 | tf_op jit(solution)/shard_map/psum | solution.py:100
  108.3 55.8 %collective-permute-start.2 = (bf16[1024,512]{1,0:T(8,128)(2,1)}, bf16[1024,512]{1,0:T(8,128)(2,1)}, u32[]{:S(2)}, u32[]{:S(2)}) collective-permute-start(bf16[1024,512]{1,0:T(8,128)(2,1)} %bitcast.12), channel_id=1, source_target_pairs={{0,28},{4,0},{8,4},{12,8},{16,12},{20,16},{24,20},{28,24},{1,29},{... | collective-permute-start | bytes 3145736 | tf_op jit(solution)/shard_map/ppermute | solution.py:11
  164.0 85.5 %reduce-scatter.6.cloned.1.call-start = ((), (), s32[]{:S(2)}) async-start(), calls=%async_computation.6 | async-start | bytes 1310720 | tf_op jit(solution)/shard_map/reduce_scatter | solution.py:70
  167.3 2.3 copy-start.3
  167.3 2.3 copy-start.7
Sparse Core Ops, SparseCore 0:
  9.6 30.6 all-gather.1
  76.7 20.3 reduce-scatter.9
  99.4 20.0 reduce-scatter.11
  121.7 20.0 reduce-scatter.7
  143.9 20.0 reduce-scatter.13
  167.2 53.3 all-reduce.2
  222.9 26.6 reduce-scatter.5
where the time goes:
time: 259 us; the launch traced here: 258 us
  waiting for transfers between devices  185 us (71%)
  other arithmetic  25 us (10%)
  local copies, waits for them, and re-layouts  16.3 us (6%)
  between operations  14.4 us (6%)
  matrix products  13.4 us (5%)
  starting transfers between devices  4.32 us (2%)
    psum x1, waiting for transfers between devices, local(): lax.psum(shares[0].astype(jnp.bfloat16), 'row').astype(jnp.float32)  50.6 us
    all_gather x1, waiting for transfers between devices, local(): own_panel = lax.all_gather(features, 'rep', axis=0, tiled=True)  32.3 us
    reduce_scatter x1, waiting for transfers between devices, local(): lax.psum_scatter((own_part + from_next + from_prior).astype(jnp.bfloat16)...  25.3 us
    ppermute x4, waiting for transfers between devices, from_behind(): return lax.ppermute(value, axis, pairs)  24.5 us
    reduce_scatter x1, waiting for transfers between devices, local(): lax.psum_scatter(local_output.astype(jnp.bfloat16), 'rep', scatter_dimens...  22.2 us
    reduce_scatter x1, waiting for transfers between devices, local(): lax.psum_scatter(local_self.astype(jnp.bfloat16), 'rep', scatter_dimensio...  22.2 us
    scatter-add x1, other arithmetic, local(): spread.at[window_index.reshape(-1)]  9.55 us
    reduce_scatter x1, waiting for transfers between devices, local(): lax.psum_scatter(local_aggregate.astype(jnp.bfloat16), 'rep', scatter_dim...  6.68 us
  transfers between devices with their start and end apart: 11, of which 8 were waited for; matrix products, arithmetic and copies ran while one was open for 17% of the time, Pallas kernels for 0%

commit v1 on v0

--- a/solution.py
+++ b/solution.py
@@ -32,7 +32,21 @@
     group_id = lax.axis_index("row")
     slot_of = (columns // panel_blocks - group_id + 1) % groups
     window_index = slot_of * panel_blocks + columns % panel_blocks
-    own_panel = lax.all_gather(features, "rep", axis=0, tiled=True)
+    world = lax.axis_size("rep")
+    series = []
+    for to_i in range(world):
+        series.append((to_i, (to_i + 1) % world))
+    nodes = []
+    for to_i in range(world):
+        nodes.append((to_i, (to_i - 1) % world))
+    spare, clean = ([features], [features])
+    for _ in range(world // 2):
+        spare.append(lax.ppermute(spare[-1], "rep", series))
+    for _ in range((world - 1) // 2):
+        back = lax.ppermute(clean[-1], "rep", nodes)
+        clean.append(back)
+    view_out = jnp.concatenate([*spare[::-1], *clean[1:]], axis=0)
+    own_panel = jnp.roll(view_out, (lax.axis_index("rep") - world // 2) * features.shape[0], axis=0)
     prior_panel = from_behind(own_panel, "row", 1)
     next_panel = from_behind(own_panel, "row", -1)
     window = jnp.concatenate([prior_panel, own_panel, next_panel], 0).reshape(

time: 259 us -> 250 us (0.965)
  waiting for transfers between devices: 185 us -> 170 us
  starting transfers between devices: 4.32 us -> 10.4 us
    all_gather x1 -> x0, waiting for transfers between devices: 32.3 us -> none  [local(): own_panel = lax.all_gather(features, 'rep', axis=0, tiled=True)]
    ppermute x0 -> x3, waiting for transfers between devices: none -> 17 us  [the longest x2 15.7 us: local(): spare.append(lax.ppermute(spare[-1], 'rep', series))]
    ppermute x0 -> x3, starting transfers between devices: none -> 6.93 us  [the longest x1 3.82 us: local(): back = lax.ppermute(clean[-1], 'rep', nodes)]
  transfers between devices with their start and end apart: 11 -> 13, of which waited for: 8 -> 10; matrix products, arithmetic and copies ran while one was open for 17% -> 17% of each run, Pallas kernels for 0% -> 0%
where the time goes in v1:
time: 250 us
  waiting for transfers between devices  170 us (68%)
  other arithmetic  24.3 us (10%)
  local copies, waits for them, and re-layouts  17.7 us (7%)
  between operations  14.4 us (6%)
  matrix products  12.4 us (5%)
  starting transfers between devices  10.4 us (4%)
    psum x1, waiting for transfers between devices, local(): lax.psum(shares[0].astype(jnp.bfloat16), 'row').astype(jnp.float32)  50.6 us
    ppermute x4, waiting for transfers between devices, from_behind(): return lax.ppermute(value, axis, pairs)  25.7 us
    reduce_scatter x1, waiting for transfers between devices, local(): lax.psum_scatter((own_part + from_next + from_prior).astype(jnp.bfloat16)...  25.2 us
    reduce_scatter x1, waiting for transfers between devices, local(): lax.psum_scatter(local_output.astype(jnp.bfloat16), 'rep', scatter_dimens...  22.4 us
    reduce_scatter x1, waiting for transfers between devices, local(): lax.psum_scatter(local_self.astype(jnp.bfloat16), 'rep', scatter_dimensio...  22.2 us
    ppermute x2, waiting for transfers between devices, local(): spare.append(lax.ppermute(spare[-1], 'rep', series))  15.7 us
    scatter-add x1, other arithmetic, local(): spread.at[window_index.reshape(-1)]  9.5 us
    reduce_scatter x1, waiting for transfers between devices, local(): lax.psum_scatter(local_aggregate.astype(jnp.bfloat16), 'rep', scatter_dim...  7.2 us
  transfers between devices with their start and end apart: 13, of which 10 were waited for; matrix products, arithmetic and copies ran while one was open for 17% of the time, Pallas kernels for 0%

profile of v1, /device:TPU:0, one launch (start us, length us, event | category | flops | bytes accessed | tf_op | source)
XLA Modules:
  0.0 249.7 jit_solution(17049789720000088475)
XLA Ops:
  7.2 0.0 copy-start
  7.2 0.0 copy-start.1
  7.2 0.0 reduce-scatter.10.cloned.1.call-start
  7.2 3.1 %collective-permute-start = (bf16[256,512]{1,0:T(8,128)(2,1)}, bf16[256,512]{1,0:T(8,128)(2,1)S(1)}, u32[]{:S(2)}, u32[]{:S(2)}) collective-permute-start(bf16[256,512]{1,0:T(8,128)(2,1)} %param.8), channel_id=1, source_target_pairs={{0,1},{1,2},{2,3},{3,0},{4,5},{5,6},{6,7},{7,4},{8,9},{9,10},{10,1... | collective-permute-start | bytes 786440 | tf_op jit(solution)/shard_map/ppermute | solution.py:44
  10.3 8.5 %collective-permute-done = bf16[256,512]{1,0:T(8,128)(2,1)S(1)} collective-permute-done((bf16[256,512]{1,0:T(8,128)(2,1)}, bf16[256,512]{1,0:T(8,128)(2,1)S(1)}, u32[]{:S(2)}, u32[]{:S(2)}) %collective-permute-start) | collective-permute-done | bytes 262176 | tf_op jit(solution)/shard_map/ppermute | solution.py:44
  18.9 3.8 %collective-permute-start.2 = (bf16[256,512]{1,0:T(8,128)(2,1)}, bf16[256,512]{1,0:T(8,128)(2,1)S(1)}, u32[]{:S(2)}, u32[]{:S(2)}) collective-permute-start(bf16[256,512]{1,0:T(8,128)(2,1)} %param.8), channel_id=1, source_target_pairs={{0,3},{1,0},{2,1},{3,2},{4,7},{5,4},{6,5},{7,6},{8,11},{9,8},{10,9... | collective-permute-start | bytes 786440 | tf_op jit(solution)/shard_map/ppermute | solution.py:46
  22.7 7.2 %collective-permute-done.1 = bf16[256,512]{1,0:T(8,128)(2,1)S(1)} collective-permute-done((bf16[256,512]{1,0:T(8,128)(2,1)S(1)}, bf16[256,512]{1,0:T(8,128)(2,1)S(1)}, u32[]{:S(2)}, u32[]{:S(2)}) %collective-permute-start.1) | collective-permute-done | bytes 262176 | tf_op jit(solution)/shard_map/ppermute | solution.py:44
  29.9 1.0 constant_dynamic-update-slice_fusion.5
  30.9 1.3 collective-permute-done.2
  32.3 0.1 constant_dynamic-slice_fusion
  32.4 0.3 collective-permute-start.4
  32.7 0.2 collective-permute-start.3
  33.0 0.1 reshape.66
  33.1 22.7 %collective-permute-done.4 = bf16[1024,512]{1,0:T(8,128)(2,1)S(1)} collective-permute-done((bf16[1024,512]{1,0:T(8,128)(2,1)S(1)}, bf16[1024,512]{1,0:T(8,128)(2,1)S(1)}, u32[]{:S(2)}, u32[]{:S(2)}) %collective-permute-start.4) | collective-permute-done | bytes 1048608 | tf_op jit(solution)/shard_map/ppermute | solution.py:11
  55.8 3.0 %collective-permute-done.3 = bf16[1024,512]{1,0:T(8,128)(2,1)} collective-permute-done((bf16[1024,512]{1,0:T(8,128)(2,1)S(1)}, bf16[1024,512]{1,0:T(8,128)(2,1)}, u32[]{:S(2)}, u32[]{:S(2)}) %collective-permute-start.3) | collective-permute-done | bytes 1048608 | tf_op jit(solution)/shard_map/ppermute | solution.py:11
  58.8 2.8 %pad_maximum_fusion = bf16[3072,512]{1,0:T(8,128)(2,1)} fusion(bf16[1024,512]{1,0:T(8,128)(2,1)S(1)} %collective-permute-done.4, bf16[1024,512]{1,0:T(8,128)(2,1)S(1)} %constant_dynamic-slice_fusion, bf16[1024,512]{1,0:T(8,128)(2,1)} %collective-permute-done.3), kind=kLoop, calls=%fused_computation.2 | loop fusion | flops 9437184 | bytes 6291456 | tf_op jit(solution)/shard_map/concatenate | solution.py:52
  61.6 2.6 %gather_fusion = bf16[16,128,512]{2,1,0:T(8,128)(2,1)S(1)} fusion(bf16[24,128,512]{2,1,0:T(8,128)(2,1)} %bitcast.55, s32[1024]{0:T(1024)S(1)} %pad_clamp_fusion), kind=kCustom, calls=%fused_computation | custom fusion | bytes 4194368 | tf_op jit(solution)/shard_map/gather | solution.py:55
  64.2 0.5 fusion.3
  64.7 0.5 copy-done.4
  65.2 0.3 fusion.14
  65.6 0.3 convolution_add_fusion.2
  65.9 0.3 fusion.11
  66.2 0.3 copy-done.6
  66.5 0.2 copy-done.10
  66.7 0.4 fusion.5
  67.1 0.4 copy-done.11
  67.5 1.2 convolution_convert_fusion.2
  68.7 0.0 reduce-scatter.10.cloned.1.call-update
  68.7 0.0 reduce-scatter.12.cloned.1.call-start
  68.8 0.4 fusion.6
  69.2 1.1 convolution_convert_fusion.1
  70.3 0.0 reduce-scatter.12.cloned.1.call-update
  70.3 0.0 reduce-scatter.8.cloned.1.call-start
  70.3 0.1 reshape.61
  70.4 1.2 convolution_convert_fusion.3
  71.6 0.0 reduce-scatter.8.cloned.1.call-update
  71.6 0.0 reduce-scatter.14.cloned.1.call-start
  71.7 0.3 convolution_convert_fusion.4
  72.0 2.7 %fusion.15 = f32[2,512,8,128]{3,1,2,0:T(8,128)} fusion(bf16[2,128,512,1]{2,1,3,0:T(8,128)(2,1)S(1)} %bitcast.59, bf16[2,8,128,128]{3,2,1,0:T(8,128)(2,1)S(1)} %copy-done), kind=kOutput, calls=%fused_computation.58 | convolution fusion | flops 268435456 | bytes 4980736 | tf_op jit(solution)/shard_map/bkji,bjf->bkif/dot_general | solution.py:75
  74.7 5.4 %copy.15 = f32[16,128,512]{2,1,0:T(8,128)} copy(f32[16,128,512]{1,2,0:T(8,128)} %bitcast.54) | data formatting | bytes 8388608 | tf_op jit(solution)/shard_map/reshape | solution.py:77
  80.1 3.5 %broadcast_in_dim.8 = f32[24,128,512]{2,1,0:T(8,128)} broadcast(f32[]{:T(128)} %constant.82.clone.1), dimensions={} | broadcast | bytes 6291460 | tf_op jit(solution)/shard_map/broadcast_in_dim | solution.py:76
  83.5 9.5 %scatter_fusion = f32[24,128,512]{2,1,0:T(8,128)} fusion(f32[24,128,512]{2,1,0:T(8,128)} %broadcast_in_dim.8, s32[16]{0:T(128)S(1)} %fusion.10, f32[16,128,512]{2,1,0:T(8,128)} %copy.15), kind=kCustom, calls=%fused_computation.1 | custom fusion | flops 1048576 | bytes 12582976 | tf_op jit(solution)/shard_map/scatter-add | solution.py:77
  93.0 3.3 %convert.4 = bf16[24,128,512]{2,1,0:T(8,128)(2,1)S(1)} convert(f32[24,128,512]{2,1,0:T(8,128)} %scatter_fusion) | non-fusion elementwise | flops 1572864 | bytes 9437184 | tf_op jit(solution)/shard_map/convert.1
  96.4 1.6 fusion.13
  98.0 1.2 fusion.2
  99.2 0.0 reduce-scatter.14.cloned.1.call-update
  99.2 0.0 all-reduce.3.cloned.1.call-start
  99.3 2.7 %collective-permute-start.5 = (bf16[1024,512]{1,0:T(8,128)(2,1)}, bf16[1024,512]{1,0:T(8,128)(2,1)}, u32[]{:S(2)}, u32[]{:S(2)}) collective-permute-start(bf16[1024,512]{1,0:T(8,128)(2,1)} %bitcast.12), channel_id=1, source_target_pairs={{0,28},{4,0},{8,4},{12,8},{16,12},{20,16},{24,20},{28,24},{1,29},{... | collective-permute-start | bytes 3145736 | tf_op jit(solution)/shard_map/ppermute | solution.py:11
  102.0 1.9 slice.22
  103.9 0.0 reduce-scatter.10.cloned.1.call-done
  103.9 7.2 %reduce-scatter.12.cloned.1.call-done = bf16[128,512]{1,0:T(8,128)(2,1)} async-done(((bf16[512,512]{1,0:T(8,128)(2,1)}), bf16[128,512]{1,0:T(8,128)(2,1)}) %reduce-scatter.12.cloned.1.call-update) | async-done | bytes 131088 | tf_op jit(solution)/shard_map/reduce_scatter | solution.py:106
  111.1 22.4 %reduce-scatter.8.cloned.1.call-done = bf16[128,512]{1,0:T(8,128)(2,1)} async-done(((bf16[512,512]{1,0:T(8,128)(2,1)}), bf16[128,512]{1,0:T(8,128)(2,1)}) %reduce-scatter.8.cloned.1.call-update) | async-done | bytes 131088 | tf_op jit(solution)/shard_map/reduce_scatter | solution.py:100
  133.5 22.2 %reduce-scatter.14.cloned.1.call-done = bf16[128,512]{1,0:T(8,128)(2,1)} async-done(((bf16[512,512]{1,0:T(8,128)(2,1)}), bf16[128,512]{1,0:T(8,128)(2,1)}) %reduce-scatter.14.cloned.1.call-update) | async-done | bytes 131088 | tf_op jit(solution)/shard_map/reduce_scatter | solution.py:109
  155.7 0.0 all-reduce.3.cloned.1.call-update
  155.8 0.0 reduce-scatter.6.cloned.1.call-start
  155.8 3.2 %fusion.1 = bf16[1024,512]{1,0:T(8,128)(2,1)} fusion(f32[8,128,512]{2,1,0:T(8,128)S(1)} %slice.22, bf16[1024,512]{1,0:T(8,128)(2,1)} %collective-permute-done.6, bf16[1024,512]{1,0:T(8,128)(2,1)} %collective-permute-done.5), kind=kLoop, calls=%fused_computation.5 | loop fusion | flops 2621440 | bytes 5242880 | tf_op jit(solution)/shard_map/convert_element_type | solution.py:85
  159.1 0.0 reduce-scatter.6.cloned.1.call-update
  159.1 2.3 fusion.4
  161.4 0.3 convolution_add_fusion
  161.7 50.6 %all-reduce.3.cloned.1.call-done = (bf16[128,512]{1,0:T(8,128)(2,1)}, bf16[128,512]{1,0:T(8,128)(2,1)}, bf16[128,512]{1,0:T(8,128)(2,1)}, bf16[128,512]{1,0:T(8,128)(2,1)}) async-done(((bf16[128,512]{1,0:T(8,128)(2,1)}, bf16[128,512]{1,0:T(8,128)(2,1)}, bf16[128,512]{1,0:T(8,128)(2,1)}, bf16[128,512]{1,0:T(8,128)(2,1)}), (bf16[128,512]{1,0:T(8,128)(2,1)}, bf16[128,512]{1,0:T(8,128)(2,1)}, ...) | async-done | bytes 524304 | tf_op jit(solution)/shard_map/psum | solution.py:114
  212.3 1.8 convert_multiply_fusion.2
  214.1 1.8 convert_multiply_fusion
  216.0 25.2 %reduce-scatter.6.cloned.1.call-done = bf16[256,512]{1,0:T(8,128)(2,1)} async-done(((bf16[1024,512]{1,0:T(8,128)(2,1)}), bf16[256,512]{1,0:T(8,128)(2,1)}) %reduce-scatter.6.cloned.1.call-update) | async-done | bytes 262160 | tf_op jit(solution)/shard_map/reduce_scatter | solution.py:84
  241.1 1.7 add_convert_fusion
  (34 shorter events, 0.2 us)
Async XLA Ops:
  7.2 57.0 %copy-start = (bf16[2,8,128,128]{3,2,1,0:T(8,128)(2,1)S(1)}, bf16[2,8,128,128]{3,2,1,0:T(8,128)(2,1)}, u32[]{:S(2)}) copy-start(bf16[2,8,128,128]{3,2,1,0:T(8,128)(2,1)} %param.9) | copy-start | bytes 1572868
  7.2 25.1 %copy-start.1 = (bf16[256,512]{1,0:T(8,128)(2,1)S(1)}, bf16[256,512]{1,0:T(8,128)(2,1)}, u32[]{:S(2)}) copy-start(bf16[256,512]{1,0:T(8,128)(2,1)} %param.8) | copy-start | bytes 786436
  7.2 96.7 %reduce-scatter.10.cloned.1.call-start = ((), (), s32[]{:S(2)}) async-start(), calls=%async_computation.7 | async-start | bytes 655360 | tf_op jit(solution)/shard_map/reduce_scatter | solution.py:103
  7.2 11.6 %collective-permute-start = (bf16[256,512]{1,0:T(8,128)(2,1)}, bf16[256,512]{1,0:T(8,128)(2,1)S(1)}, u32[]{:S(2)}, u32[]{:S(2)}) collective-permute-start(bf16[256,512]{1,0:T(8,128)(2,1)} %param.8), channel_id=1, source_target_pairs={{0,1},{1,2},{2,3},{3,0},{4,5},{5,6},{6,7},{7,4},{8,9},{9,10},{10,1... | collective-permute-start | bytes 786440 | tf_op jit(solution)/shard_map/ppermute | solution.py:44
  18.9 11.0 %collective-permute-start.1 = (bf16[256,512]{1,0:T(8,128)(2,1)S(1)}, bf16[256,512]{1,0:T(8,128)(2,1)S(1)}, u32[]{:S(2)}, u32[]{:S(2)}) collective-permute-start(bf16[256,512]{1,0:T(8,128)(2,1)S(1)} %collective-permute-done), channel_id=1, source_target_pairs={{0,1},{1,2},{2,3},{3,0},{4,5},{5,6},{6,7},{7,4},{8,9},{9,10},{10,1... | collective-permute-start | bytes 786440 | tf_op jit(solution)/shard_map/ppermute | solution.py:44
  18.9 13.3 %collective-permute-start.2 = (bf16[256,512]{1,0:T(8,128)(2,1)}, bf16[256,512]{1,0:T(8,128)(2,1)S(1)}, u32[]{:S(2)}, u32[]{:S(2)}) collective-permute-start(bf16[256,512]{1,0:T(8,128)(2,1)} %param.8), channel_id=1, source_target_pairs={{0,3},{1,0},{2,1},{3,2},{4,7},{5,4},{6,5},{7,6},{8,11},{9,8},{10,9... | collective-permute-start | bytes 786440 | tf_op jit(solution)/shard_map/ppermute | solution.py:46
  32.2 0.8 copy-start.8
  32.4 23.4 %collective-permute-start.4 = (bf16[1024,512]{1,0:T(8,128)(2,1)S(1)}, bf16[1024,512]{1,0:T(8,128)(2,1)S(1)}, u32[]{:S(2)}, u32[]{:S(2)}) collective-permute-start(bf16[1024,512]{1,0:T(8,128)(2,1)S(1)} %constant_dynamic-slice_fusion), channel_id=1, source_target_pairs={{0,28},{4,0},{8,4},{12,8},{16,12},{20,16},{24,20},{28,24},{1,29},{... | collective-permute-start | bytes 3145736 | tf_op jit(solution)/shard_map/ppermute | solution.py:11
  32.7 26.1 %collective-permute-start.3 = (bf16[1024,512]{1,0:T(8,128)(2,1)S(1)}, bf16[1024,512]{1,0:T(8,128)(2,1)}, u32[]{:S(2)}, u32[]{:S(2)}) collective-permute-start(bf16[1024,512]{1,0:T(8,128)(2,1)S(1)} %constant_dynamic-slice_fusion), channel_id=1, source_target_pairs={{0,4},{4,8},{8,12},{12,16},{16,20},{20,24},{24,28},{28,0},{1,5},{5... | collective-permute-start | bytes 3145736 | tf_op jit(solution)/shard_map/ppermute | solution.py:11
  64.2 1.0 copy-start.4
  64.2 1.3 copy-start.2
  64.7 1.2 copy-start.9
  65.6 1.0 copy-start.6
  65.6 1.1 copy-start.10
  66.7 0.8 copy-start.11
  68.7 1.7 copy-start.12
  68.7 42.4 %reduce-scatter.12.cloned.1.call-start = ((), (), s32[]{:S(2)}) async-start(), calls=%async_computation.8 | async-start | bytes 655360 | tf_op jit(solution)/shard_map/reduce_scatter | solution.py:106
  70.3 1.4 copy-start.5
  70.3 63.2 %reduce-scatter.8.cloned.1.call-start = ((), (), s32[]{:S(2)}) async-start(), calls=%async_computation.6 | async-start | bytes 655360 | tf_op jit(solution)/shard_map/reduce_scatter | solution.py:100
  71.6 84.1 %reduce-scatter.14.cloned.1.call-start = ((), (), s32[]{:S(2)}) async-start(), calls=%async_computation.9 | async-start | bytes 655360 | tf_op jit(solution)/shard_map/reduce_scatter | solution.py:109
  98.0 57.8 %collective-permute-start.6 = (bf16[1024,512]{1,0:T(8,128)(2,1)}, bf16[1024,512]{1,0:T(8,128)(2,1)}, u32[]{:S(2)}, u32[]{:S(2)}) collective-permute-start(bf16[1024,512]{1,0:T(8,128)(2,1)} %bitcast.13), channel_id=1, source_target_pairs={{0,4},{4,8},{8,12},{12,16},{16,20},{20,24},{24,28},{28,0},{1,5},{5... | collective-permute-start | bytes 3145736 | tf_op jit(solution)/shard_map/ppermute | solution.py:11
  99.2 113.1 %all-reduce.3.cloned.1.call-start = ((), (), s32[]{:S(2)}) async-start(), calls=%async_computation.10 | async-start | bytes 1048576 | tf_op jit(solution)/shard_map/psum | solution.py:114
  99.3 56.6 %collective-permute-start.5 = (bf16[1024,512]{1,0:T(8,128)(2,1)}, bf16[1024,512]{1,0:T(8,128)(2,1)}, u32[]{:S(2)}, u32[]{:S(2)}) collective-permute-start(bf16[1024,512]{1,0:T(8,128)(2,1)} %bitcast.12), channel_id=1, source_target_pairs={{0,28},{4,0},{8,4},{12,8},{16,12},{20,16},{24,20},{28,24},{1,29},{... | collective-permute-start | bytes 3145736 | tf_op jit(solution)/shard_map/ppermute | solution.py:11
  155.8 85.4 %reduce-scatter.6.cloned.1.call-start = ((), (), s32[]{:S(2)}) async-start(), calls=%async_computation.5 | async-start | bytes 1310720 | tf_op jit(solution)/shard_map/reduce_scatter | solution.py:84
  159.1 2.3 copy-start.3
  159.1 2.3 copy-start.7
Sparse Core Ops, SparseCore 0:
  68.8 19.7 reduce-scatter.9
  90.9 20.1 reduce-scatter.11
  113.4 20.0 reduce-scatter.7
  135.6 20.0 reduce-scatter.13
  158.9 53.3 all-reduce.2
  214.5 26.6 reduce-scatter.5
